TPU v7x, 32 devices: a whole 2x2x4 slice. The times are simulated.
32 devices in a mesh: groups: 2 (over y), seq: 2 (over core), mp: 8 (over z, x).
Axes of the slice: x: 2, y: 2, z: 4, core: 2. Of those that a mesh axis runs over, the one named last changes fastest.
Arguments:
- residual: bfloat16 [1024, 5376], P(('groups', 'seq', 'mp')), parts along dimension 0, may hold values from -6 to 6
- positions: int32 [1024], P(('groups', 'seq')), parts along dimension 0, may hold values from 0 to 383, as said below
- window_start: int32 [1024], P(('groups', 'seq')), parts along dimension 0, may hold values from 0 to 448, as said below
- input_gain: float32 [5376], replicated, may hold values from 0.1 to 1.9
- attention_gain: float32 [5376], replicated, may hold values from 0.1 to 1.9
- feedforward_gain: float32 [5376], replicated, may hold values from 0.1 to 1.9
- output_gain: float32 [5376], replicated, may hold values from 0.1 to 1.9
- query_weight: bfloat16 [5376, 4096], P(None, 'mp'), may hold values from -0.078125 to 0.078125
- key_weight: bfloat16 [5376, 2048], P(None, 'mp'), may hold values from -0.078125 to 0.078125
- value_weight: bfloat16 [5376, 2048], P(None, 'mp'), may hold values from -0.078125 to 0.078125
- output_weight: bfloat16 [4096, 5376], P('mp'), may hold values from -0.09375 to 0.09375
- gate_weight: bfloat16 [5376, 21504], P(None, 'mp'), may hold values from -0.078125 to 0.078125
- up_weight: bfloat16 [5376, 21504], P(None, 'mp'), may hold values from -0.078125 to 0.078125
- down_weight: bfloat16 [21504, 5376], P('mp'), may hold values from -0.0390625 to 0.0390625
Outputs:
- layer_out: bfloat16 [1024, 5376], P(('groups', 'seq', 'mp')), parts along dimension 0
There are 2 independent parts, one for each index of `groups`. A program takes and returns all parts, laid end to end along the dimension named above; an argument that names none is the same for every part. Nothing has to cross between parts.
Inputs may be any that keep to these rules, and one draw needn't show every extreme that they name: positions[i] is i minus the first row of the document that holds row i; documents are consecutive runs of rows; one document of exactly 384 rows starts before row 32, the rows before it and the rows after it up to row 448 form shorter documents, and the last document starts at row 448. window_start[i] = max(first row of the document that holds row i, i - 191).
All inputs are finite; a program needn't handle non-finite values.
Results may differ from a plain program's by a relative error of at most 0.02.
Values may be sent and summed in bfloat16 or wider, within the bound.
A program may use at most 192 MiB of HBM per device.

v0:
```python
import jax
import jax.numpy as jnp
from jax import lax
from jax.sharding import PartitionSpec as P

D = 5376
FF = 21504
QH = 32
HD = 128
WAL = 64


epsilon = 1e-06


def partner(block, axis, apart):
    count = lax.axis_size(axis)
    route = []
    for low in range(count):
        high = low | 1 << apart
        if high != low and high < count:
            route += [(low, high), (high, low)]
    return lax.ppermute(block, axis, route)


def for_sending(value):
    return jax.tree.map(lambda a: a.astype(jnp.bfloat16) if a.dtype == jnp.float32 else a, value)


def from_behind(block, axis, distance):
    devices = range(lax.axis_size(axis))
    route = [(i - distance, i) for i in devices if i - distance in devices]
    return lax.ppermute(block, axis, route)


def normalize(values_in, gain_row):
    widened = values_in.astype(jnp.float32)
    mean_square = jnp.mean(widened * widened, axis=-1, keepdims=True)
    return widened * lax.rsqrt(mean_square + epsilon) * gain_row


def walsh_table(length):
    row_index = lax.broadcasted_iota(jnp.int32, (length, length), 0)
    column_index = lax.broadcasted_iota(jnp.int32, (length, length), 1)
    common = jnp.bitwise_and(row_index, column_index)
    parity = jnp.zeros((length, length), jnp.int32)
    for offset in range(max(length.bit_length() - 1, 0)):
        parity = parity + jnp.bitwise_and(jnp.right_shift(common, offset), 1)
    return (1 - 2 * jnp.bitwise_and(parity, 1)).astype(jnp.float32)


def angle_tables(positions, head_size):
    half_size = head_size // 2
    inverse = jnp.power(10000.0, -jnp.arange(half_size, dtype=jnp.float32) / half_size)
    angles = positions.astype(jnp.float32)[:, None] * inverse[None, :]
    return (jnp.cos(angles), jnp.sin(angles))


def rotary(linear, cosine_table, sine_table):
    row_count = linear.shape[0]
    half_size = cosine_table.shape[1]
    split_heads = linear.astype(jnp.float32).reshape(row_count, -1, 2 * half_size)
    front_half = split_heads[:, :, :half_size]
    back_half = split_heads[:, :, half_size:]
    cos_rows = cosine_table[:, None, :]
    sin_rows = sine_table[:, None, :]
    turned = jnp.concatenate(
        [
            front_half * cos_rows - back_half * sin_rows,
            back_half * cos_rows + front_half * sin_rows,
        ],
        axis=-1,
    )
    return turned.reshape(row_count, -1)


def join_pair(own_part, theirs, upper_bit, axis_number):
    lower_part = jnp.where(upper_bit == 1, theirs, own_part)
    upper_part = jnp.where(upper_bit == 1, own_part, theirs)
    return jnp.concatenate([lower_part, upper_part], axis=axis_number)


def attend(queries, key_rows, value_rows, allowed):
    scores = jnp.einsum("qgtd,kgd->gtqk", queries, key_rows, preferred_element_type=jnp.float32)
    scores = jnp.where(allowed[None, None], scores, -1e30)
    largest = jnp.max(scores, axis=-1, keepdims=True)
    exponent = jnp.exp(scores - largest)
    probabilities = (exponent / jnp.sum(exponent, axis=-1, keepdims=True)).astype(jnp.bfloat16)
    combined = jnp.einsum(
        "gtqk,kgd->qgtd", probabilities, value_rows, preferred_element_type=jnp.float32
    )
    return combined.astype(jnp.bfloat16)


def body(
    residual,
    positions,
    window_start,
    input_gain,
    attention_gain,
    feedforward_gain,
    output_gain,
    query_weight,
    key_weight,
    value_weight,
    output_weight,
    gate_weight,
    up_weight,
    down_weight,
):
    model_count = lax.axis_size("mp")
    model_index = lax.axis_index("mp")
    block_index = lax.axis_index("seq")
    block_input = lax.all_gather(residual, "mp", axis=0, tiled=True)
    block_length = block_input.shape[0]
    own_rows = block_length // model_count
    model_width = output_weight.shape[1]
    normed = normalize(block_input, input_gain).astype(jnp.bfloat16)
    cosine_table, sine_table = angle_tables(positions, HD)
    query_scale = float(D // QH) ** (-0.5)
    paired = model_count == 2 * QH
    if paired:
        half_rows = block_length // 2
        quarter_rows = block_length // 4
        low_bit = model_index % 2
        query_first = low_bit * half_rows
        query_cosine = lax.dynamic_slice_in_dim(cosine_table, query_first, half_rows, 0)
        query_sine = lax.dynamic_slice_in_dim(sine_table, query_first, half_rows, 0)
        partner_columns = partner(query_weight, "mp", 0)
        full_query = join_pair(query_weight, partner_columns, low_bit, 1)
        query_normed = lax.dynamic_slice_in_dim(normed, query_first, half_rows, 0)
        query_linear = jnp.dot(query_normed, full_query, preferred_element_type=jnp.float32).astype(
            jnp.bfloat16
        )
        key_full = key_weight
        value_full = value_weight
        for bit_number in range(2):
            upper_bit = jnp.right_shift(model_index, bit_number) % 2
            partner_key, partner_value = (
                partner(for_sending(key_full), "mp", bit_number).astype(key_full.dtype),
                partner(for_sending(value_full), "mp", bit_number).astype(value_full.dtype),
            )
            key_full = join_pair(key_full, partner_key, upper_bit, 1)
            value_full = join_pair(value_full, partner_value, upper_bit, 1)
        quarter_first = model_index % 4 * quarter_rows
        quarter_normed = lax.dynamic_slice_in_dim(normed, quarter_first, quarter_rows, 0)
        quarter_cosine = lax.dynamic_slice_in_dim(cosine_table, quarter_first, quarter_rows, 0)
        quarter_sine = lax.dynamic_slice_in_dim(sine_table, quarter_first, quarter_rows, 0)
        key_linear = jnp.dot(quarter_normed, key_full, preferred_element_type=jnp.float32).astype(
            jnp.bfloat16
        )
        key_part = rotary(key_linear, quarter_cosine, quarter_sine).astype(jnp.bfloat16)
        value_part = jnp.dot(quarter_normed, value_full, preferred_element_type=jnp.float32).astype(
            jnp.bfloat16
        )
        for bit_number in range(2):
            upper_bit = jnp.right_shift(model_index, bit_number) % 2
            partner_key, partner_value = (
                partner(for_sending(key_part), "mp", bit_number).astype(key_part.dtype),
                partner(for_sending(value_part), "mp", bit_number).astype(value_part.dtype),
            )
            key_part = join_pair(key_part, partner_key, upper_bit, 0)
            value_part = join_pair(value_part, partner_value, upper_bit, 0)
        key_rows = key_part
        value_rows = value_part
        group_count = 1
        query_count = half_rows
        queries = (rotary(query_linear, query_cosine, query_sine) * query_scale).astype(
            jnp.bfloat16
        )
        queries = queries.reshape(query_count, 1, 1, HD)
        own_window = lax.dynamic_slice_in_dim(window_start, query_first, half_rows, 0)
    else:
        query_first = 0
        query_count = block_length
        group_count = key_weight.shape[1] // HD
        query_linear = jnp.dot(normed, query_weight, preferred_element_type=jnp.float32).astype(
            jnp.bfloat16
        )
        key_linear = jnp.dot(normed, key_weight, preferred_element_type=jnp.float32).astype(
            jnp.bfloat16
        )
        key_rows = rotary(key_linear, cosine_table, sine_table).astype(jnp.bfloat16)
        value_rows = jnp.dot(normed, value_weight, preferred_element_type=jnp.float32).astype(
            jnp.bfloat16
        )
        queries = (rotary(query_linear, cosine_table, sine_table) * query_scale).astype(
            jnp.bfloat16
        )
        queries = queries.reshape(query_count, group_count, 2, HD)
        own_window = window_start
    previous_key, previous_value = from_behind((key_rows, value_rows), "seq", 1)
    all_keys = jnp.concatenate([previous_key, key_rows], axis=0).reshape(
        2 * block_length, group_count, HD
    )
    all_values = jnp.concatenate([previous_value, value_rows], axis=0).reshape(
        2 * block_length, group_count, HD
    )
    key_index = (block_index - 1) * block_length + jnp.arange(2 * block_length, dtype=jnp.int32)
    query_index = (
        block_index * block_length + query_first + jnp.arange(query_count, dtype=jnp.int32)
    )
    allowed = (key_index[None, :] <= query_index[:, None]) & (
        key_index[None, :] >= own_window[:, None]
    )
    attended = attend(queries, all_keys, all_values, allowed)
    head_walsh = walsh_table(HD).astype(jnp.bfloat16)
    rotated = jnp.einsum(
        "qgtd,de->qgte", attended, head_walsh, preferred_element_type=jnp.float32
    ) * float(HD) ** (-0.5)
    rotated = rotated.astype(jnp.bfloat16).reshape(query_count, -1)
    if paired:
        partner_rows = partner(output_weight, "mp", 0)
        full_output = join_pair(output_weight, partner_rows, low_bit, 0)
        half_term = jnp.dot(rotated, full_output, preferred_element_type=jnp.float32)
        padded = lax.dynamic_update_slice_in_dim(
            jnp.zeros((block_length, model_width), jnp.float32), half_term, query_first, 0
        )

        def attention_term(first_row, row_count):
            return lax.dynamic_slice_in_dim(padded, first_row, row_count, 0)

    else:

        def attention_term(first_row, row_count):
            picked = lax.dynamic_slice_in_dim(rotated, first_row, row_count, 0)
            return jnp.dot(picked, output_weight, preferred_element_type=jnp.float32)

    attention_rows = lax.psum_scatter(
        attention_term(jnp.int32(0), lax.axis_size("mp") * own_rows),
        "mp",
        scatter_dimension=0,
        tiled=True,
    )
    first_sum = (residual.astype(jnp.float32) + normalize(attention_rows, attention_gain)).astype(
        jnp.bfloat16
    )
    feed_own = normalize(first_sum, feedforward_gain).astype(jnp.bfloat16)
    feed_input = lax.all_gather(feed_own, "mp", axis=0, tiled=True)
    gate_out = jnp.dot(feed_input, gate_weight, preferred_element_type=jnp.float32)
    up_out = jnp.dot(feed_input, up_weight, preferred_element_type=jnp.float32)
    activated = (jax.nn.gelu(gate_out, approximate=True) * up_out).astype(jnp.bfloat16)
    local_count = WAL // model_count
    block_width = FF // WAL
    grouped = activated.reshape(block_length, local_count, block_width)
    walsh_scale = float(WAL) ** (-0.5)
    full_table = walsh_table(WAL).astype(jnp.bfloat16)
    mixed_rows = (
        jnp.einsum(
            "rab,ac->rcb",
            lax.all_to_all(grouped, "mp", split_axis=0, concat_axis=1, tiled=True),
            full_table,
            preferred_element_type=jnp.float32,
        )
        * walsh_scale
    )
    spread = lax.all_to_all(
        mixed_rows.astype(jnp.bfloat16), "mp", split_axis=1, concat_axis=0, tiled=True
    )
    spread = spread.reshape(block_length, -1)
    picked = spread
    down_rows = lax.psum_scatter(
        jnp.dot(picked, down_weight, preferred_element_type=jnp.float32),
        "mp",
        scatter_dimension=0,
        tiled=True,
    )
    return (first_sum.astype(jnp.float32) + normalize(down_rows, output_gain)).astype(jnp.bfloat16)


def solution(mesh):
    placed = (
        P(("groups", "seq", "mp"), None),
        P(("groups", "seq")),
        P(("groups", "seq")),
        P(),
        P(),
        P(),
        P(),
        P(None, "mp"),
        P(None, "mp"),
        P(None, "mp"),
        P("mp", None),
        P(None, "mp"),
        P(None, "mp"),
        P("mp", None),
    )
    return jax.shard_map(
        body,
        mesh=mesh,
        in_specs=placed,
        out_specs=P(("groups", "seq", "mp"), None),
        check_vma=False,
    )
```

profile of v0, /device:TPU:0, one launch (start us, length us, event | category | flops | bytes accessed | tf_op | source)
XLA Modules:
  0.0 507.5 jit_solution(12814948840492987857)
XLA Ops:
  6.5 0.7 all-gather.3.cloned.1.call-update
  7.3 0.7 convert_element_type.85
  8.6 0.7 copy.60
  10.0 1.5 compare_and_fusion
  11.5 56.8 %all-gather.3.cloned.1.call-done = bf16[256,5376]{1,0:T(8,128)(2,1)} async-done(((bf16[32,5376]{1,0:T(8,128)(2,1)}), bf16[256,5376]{1,0:T(8,128)(2,1)}) %all-gather.3.cloned.1.call-update) | async-done | bytes 2752528 | tf_op jit(solution)/shard_map/all_gather | solution.py:114
  68.3 2.6 fusion.1
  70.9 5.1 fusion.19
  75.9 1.2 copy.62
  77.2 0.8 fusion.64
  78.0 3.4 convolution_convert_fusion.2
  81.5 0.9 convolution_convert_fusion.3
  82.5 1.3 collective-permute-start
  83.9 1.3 collective-permute-start.1
  86.5 0.9 fusion.65
  87.9 6.6 %fusion.66 = f32[256,5376]{1,0:T(8,128)} fusion(bf16[256,512]{0,1:T(8,128)(2,1)S(1)} %bitcast.74, bf16[512,5376]{1,0:T(8,128)(2,1)} %param.24), kind=kOutput, calls=%fused_computation.98 | convolution fusion | flops 1409286144 | bytes 11272192 | tf_op jit(solution)/shard_map/dot_general | solution.py:227
  94.6 105.7 %reduce-scatter.3.cloned.1.call-done = f32[32,5376]{1,0:T(8,128)} async-done(((f32[256,5376]{1,0:T(8,128)}), f32[32,5376]{1,0:T(8,128)}) %reduce-scatter.3.cloned.1.call-update) | async-done | bytes 688144 | tf_op jit(solution)/shard_map/reduce_scatter | solution.py:229
  200.3 1.3 multiply_reduce_fusion.1
  201.5 1.4 fusion.23
  203.0 0.9 fusion.25
  204.1 55.3 %all-gather.5.cloned.1.call-done = bf16[256,5376]{1,0:T(8,128)(2,1)} async-done(((bf16[32,5376]{1,0:T(8,128)(2,1)}), bf16[256,5376]{1,0:T(8,128)(2,1)}) %all-gather.5.cloned.1.call-update) | async-done | bytes 2752528 | tf_op jit(solution)/shard_map/all_gather | solution.py:239
  259.4 17.0 %fusion.67 = f32[256,2688]{1,0:T(8,128)S(1)} fusion(bf16[256,5376]{1,0:T(8,128)(2,1)} %all-gather.5.cloned.1.call-done, bf16[5376,2688]{1,0:T(8,128)(2,1)} %param.25), kind=kOutput, calls=%fused_computation.99 | convolution fusion | flops 7398752256 | bytes 34406400 | tf_op jit(solution)/shard_map/dot_general | solution.py:240
  276.5 14.2 %fusion.4 = bf16[256,2688]{1,0:T(8,128)(2,1)S(1)} fusion(bf16[256,5376]{1,0:T(8,128)(2,1)S(1)} %copy-done.14, bf16[5376,2688]{1,0:T(8,128)(2,1)} %param.26, f32[256,2688]{1,0:T(8,128)S(1)} %fusion.67), kind=kOutput, calls=%fused_computation.8 | convolution fusion | flops 7405633536 | bytes 35782656 | tf_op jit(solution)/shard_map/dot_general | solution.py:241
  290.8 0.8 copy.69
  291.6 1.3 copy.70
  292.9 39.8 %all_to_all.33 = bf16[256,8,336]{2,1,0:T(8,128)(2,1)S(1)} all-to-all(bf16[256,8,336]{2,1,0:T(8,128)(2,1)S(1)} %copy.70), channel_id=1, replica_groups=mesh['groups'=2,'seq'=2,'mp'=8] {'mp'}, dimensions={0} | all-to-all | bytes 2752512 | tf_op jit(solution)/shard_map/all_to_all | solution.py:251
  333.2 0.9 copy.72
  334.2 40.0 %all_to_all.34 = bf16[32,64,336]{2,0,1:T(8,128)(2,1)S(1)} all-to-all(bf16[32,64,336]{2,0,1:T(8,128)(2,1)S(1)} %copy.72), channel_id=1, replica_groups=mesh['groups'=2,'seq'=2,'mp'=8] {'mp'}, dimensions={1} | all-to-all | bytes 2752512 | tf_op jit(solution)/shard_map/all_to_all | solution.py:257
  374.8 1.3 reshape.195
  376.1 16.0 %fusion.68 = f32[256,5376]{1,0:T(8,128)} fusion(bf16[256,2688]{1,0:T(8,128)(2,1)S(1)} %reshape.195, bf16[2688,5376]{1,0:T(8,128)(2,1)} %param.27), kind=kOutput, calls=%fused_computation.100 | convolution fusion | flops 7398752256 | bytes 35782656 | tf_op jit(solution)/shard_map/dot_general | solution.py:263
  392.2 105.5 %reduce-scatter.5.cloned.1.call-done = f32[32,5376]{1,0:T(8,128)} async-done(((f32[256,5376]{1,0:T(8,128)}), f32[32,5376]{1,0:T(8,128)}) %reduce-scatter.5.cloned.1.call-update) | async-done | bytes 688144 | tf_op jit(solution)/shard_map/reduce_scatter | solution.py:262
  497.7 1.3 multiply_reduce_fusion
  499.0 2.0 fusion.26
  (65 shorter events, 4.7 us)
Async XLA Ops:
  6.5 71.5 %copy-start = (bf16[5376,256]{1,0:T(8,128)(2,1)S(1)}, bf16[5376,256]{1,0:T(8,128)(2,1)}, u32[]{:S(2)}) copy-start(bf16[5376,256]{1,0:T(8,128)(2,1)} %param.22) | copy-start | bytes 8257540
  6.5 64.3 %copy-start.15 = (f32[5376]{0:T(1024)S(1)}, f32[5376]{0:T(1024)}, u32[]{:S(2)}) copy-start(f32[5376]{0:T(1024)} %param.17) | copy-start | bytes 64516
  6.5 61.7 %all-gather.3.cloned.1.call-start = ((), (), s32[]{:S(2)}) async-start(), calls=%async_computation.4 | async-start | bytes 3096576 | tf_op jit(solution)/shard_map/all_gather | solution.py:114
  7.3 193.0 %reduce-scatter.3.cloned.1.call-start = ((), (), s32[]{:S(2)}) async-start(), calls=%async_computation.5 | async-start | bytes 6193152 | tf_op jit(solution)/shard_map/reduce_scatter | solution.py:229
  68.3 2.6 copy-start.2
  78.0 3.4 copy-start.3
  78.0 3.5 copy-start.13
  78.0 3.5 copy-start.16
  81.5 2.3 copy-start.7
  81.5 2.3 copy-start.8
  81.5 3.7 copy-start.6
  81.5 3.9 copy-start.5
  82.5 3.5 collective-permute-start
  83.9 2.3 collective-permute-start.1
  85.6 0.9 copy-start.9
  94.5 107.0 %copy-start.4 = (bf16[32,5376]{1,0:T(8,128)(2,1)S(1)}, bf16[32,5376]{1,0:T(8,128)(2,1)}, u32[]{:S(2)}) copy-start(bf16[32,5376]{1,0:T(8,128)(2,1)} %param.14) | copy-start | bytes 1032196
  94.5 107.0 %copy-start.11 = (f32[5376]{0:T(1024)S(1)}, f32[5376]{0:T(1024)}, u32[]{:S(2)}) copy-start(f32[5376]{0:T(1024)} %param.18) | copy-start | bytes 64516
  94.5 108.4 %copy-start.10 = (f32[5376]{0:T(1024)S(1)}, f32[5376]{0:T(1024)}, u32[]{:S(2)}) copy-start(f32[5376]{0:T(1024)} %param.19) | copy-start | bytes 64516
  94.5 164.9 %all-gather.5.cloned.1.call-start = ((), (), s32[]{:S(2)}) async-start(), calls=%async_computation.6 | async-start | bytes 3096576 | tf_op jit(solution)/shard_map/all_gather | solution.py:239
  203.9 293.8 %reduce-scatter.5.cloned.1.call-start = ((), (), s32[]{:S(2)}) async-start(), calls=%async_computation.7 | async-start | bytes 6193152 | tf_op jit(solution)/shard_map/reduce_scatter | solution.py:262
  259.4 17.1 %copy-start.14 = (bf16[256,5376]{1,0:T(8,128)(2,1)S(1)}, bf16[256,5376]{1,0:T(8,128)(2,1)}, u32[]{:S(2)}) copy-start(bf16[256,5376]{1,0:T(8,128)(2,1)} %all-gather.5.cloned.1.call-done) | copy-start | bytes 8257540
  392.1 108.8 %copy-start.1 = (bf16[5376,256]{1,0:T(8,128)(2,1)S(1)}, bf16[5376,256]{1,0:T(8,128)(2,1)}, u32[]{:S(2)}) copy-start(bf16[5376,256]{1,0:T(8,128)(2,1)} %param.22) | copy-start | bytes 8257540
  392.1 106.8 %copy-start.12 = (f32[5376]{0:T(1024)S(1)}, f32[5376]{0:T(1024)}, u32[]{:S(2)}) copy-start(f32[5376]{0:T(1024)} %param.20) | copy-start | bytes 64516
Sparse Core Ops, SparseCore 0:
  9.5 58.7 all-gather.2
  94.7 105.5 reduce-scatter.2
  204.0 55.3 all-gather.4
  392.3 105.3 reduce-scatter.4
where the time goes:
time: 508 us; the launch traced here: 507 us
  waiting for transfers between devices  324 us (64%)
  blocking collectives  79.8 us (16%)
  matrix products  65.3 us (13%)
  between operations  13.5 us (3%)
  other arithmetic  12.6 us (2%)
  local copies, waits for them, and re-layouts  9.36 us (2%)
    reduce_scatter x1, waiting for transfers between devices, body(): lax.psum_scatter(attention_term(jnp.int32(0), lax.axis_size('mp') * own_r...  106 us
    reduce_scatter x1, waiting for transfers between devices, body(): lax.psum_scatter(jnp.dot(picked, down_weight, preferred_element_type=jnp....  106 us
    all_gather x1, waiting for transfers between devices, body(): block_input = lax.all_gather(residual, 'mp', axis=0, tiled=True)  56.8 us
    all_gather x1, waiting for transfers between devices, body(): feed_input = lax.all_gather(feed_own, 'mp', axis=0, tiled=True)  55.3 us
    all_to_all x1, blocking collectives, body(): lax.all_to_all(mixed_rows.astype(jnp.bfloat16), 'mp', split_axis=1, conca...  40 us
    all_to_all x1, blocking collectives, body(): lax.all_to_all(grouped, 'mp', split_axis=0, concat_axis=1, tiled=True)  39.8 us
    dot_general x1, matrix products, body(): jnp.dot(feed_input, gate_weight, preferred_element_type=jnp.float32)  17 us
    dot_general x1, matrix products, body(): jnp.dot(picked, down_weight, preferred_element_type=jnp.float32)  16 us
  transfers between devices with their start and end apart: 6, of which 4 were waited for; matrix products, arithmetic and copies ran while one was open for 1% of the time, Pallas kernels for 0%

commit v1 on v0

--- a/solution.py
+++ b/solution.py
@@ -1,6 +1,10 @@
+import functools
+
 import jax
 import jax.numpy as jnp
 from jax import lax
+from jax.experimental import pallas as pl
+from jax.experimental.pallas import tpu as pltpu
 from jax.sharding import PartitionSpec as P
 
 D = 5376
@@ -11,6 +15,274 @@
 
 
 epsilon = 1e-06
+
+
+MESH = pl.DeviceIdType.MESH
+
+
+def block_of(ref, index, rows):
+    return ref.at[pl.ds(pl.multiple_of(index * rows, rows), rows)]
+
+
+def send(source, target, send_sem, recv_sem, device):
+    return pltpu.make_async_remote_copy(
+        src_ref=source,
+        dst_ref=target,
+        send_sem=send_sem,
+        recv_sem=recv_sem,
+        device_id={"mp": device},
+        device_id_type=MESH,
+    )
+
+
+def place(count):
+    me = lax.axis_index("mp")
+    column = lax.rem(me, 2)
+    line = lax.div(me, 2)
+    return me, column, line, count // 2, me + 1 - 2 * column
+
+
+def greet(me, line, lines, peer):
+    barrier = pltpu.get_barrier_semaphore()
+    pl.semaphore_signal(barrier, inc=1, device_id={"mp": peer}, device_id_type=MESH)
+
+    @pl.when(line > 0)
+    def _():
+        pl.semaphore_signal(barrier, inc=1, device_id={"mp": me - 2}, device_id_type=MESH)
+
+    @pl.when(line < lines - 1)
+    def _():
+        pl.semaphore_signal(barrier, inc=1, device_id={"mp": me + 2}, device_id_type=MESH)
+
+    beside = jnp.minimum(line, 1) + jnp.minimum(lines - 1 - line, 1)
+    pl.semaphore_wait(barrier, 1 + beside)
+
+
+def gather_kernel(count, own_ref, all_ref, xs, xr, us, ur, ds, dr):
+    rows = own_ref.shape[0]
+    me, column, line, lines, peer = place(count)
+    greet(me, line, lines, peer)
+
+    def across(origin, source):
+        there = block_of(all_ref, origin * 2 + column, rows)
+        return send(source, there, xs.at[origin], xr.at[origin], peer)
+
+    def upward(origin, source):
+        there = block_of(all_ref, origin * 2 + column, rows)
+        return send(source, there, us.at[origin], ur.at[origin], me + 2)
+
+    def downward(origin, source):
+        there = block_of(all_ref, origin * 2 + column, rows)
+        return send(source, there, ds.at[origin], dr.at[origin], me - 2)
+
+    @pl.when(line < lines - 1)
+    def _():
+        upward(line, own_ref).start()
+
+    @pl.when(line > 0)
+    def _():
+        downward(line, own_ref).start()
+
+    across(line, own_ref).start()
+    all_ref[pl.ds(pl.multiple_of(me * rows, rows), rows), :] = own_ref[...]
+    for step in range(1, lines):
+
+        @pl.when(line - step >= 0)
+        def _():
+            origin = line - step
+            held = block_of(all_ref, origin * 2 + column, rows)
+            upward(origin, held).wait_recv()
+
+            @pl.when(line < lines - 1)
+            def _():
+                upward(origin, held).start()
+
+            across(origin, held).start()
+
+        @pl.when(line + step < lines)
+        def _():
+            origin = line + step
+            held = block_of(all_ref, origin * 2 + column, rows)
+            downward(origin, held).wait_recv()
+
+            @pl.when(line > 0)
+            def _():
+                downward(origin, held).start()
+
+            across(origin, held).start()
+
+    for origin in range(lines):
+        across(origin, own_ref).wait_send()
+        there = block_of(all_ref, origin * 2 + 1 - column, rows)
+        send(own_ref, there, xs.at[origin], xr.at[origin], peer).wait_recv()
+
+        @pl.when((origin <= line) & (line < lines - 1))
+        def _():
+            upward(origin, own_ref).wait_send()
+
+        @pl.when((origin >= line) & (line > 0))
+        def _():
+            downward(origin, own_ref).wait_send()
+
+
+def gather_rows(own):
+    count = lax.axis_size("mp")
+    rows, width = own.shape
+    if rows % 16 or count % 2 or count < 4:
+        return lax.all_gather(own, "mp", axis=0, tiled=True)
+    lines = count // 2
+    return pl.pallas_call(
+        functools.partial(gather_kernel, count),
+        out_shape=jax.ShapeDtypeStruct((count * rows, width), own.dtype),
+        in_specs=[pl.BlockSpec(memory_space=pltpu.VMEM)],
+        out_specs=pl.BlockSpec(memory_space=pltpu.VMEM),
+        scratch_shapes=[pltpu.SemaphoreType.DMA((lines,))] * 6,
+        compiler_params=pltpu.CompilerParams(
+            collective_id=0, has_side_effects=True, vmem_limit_bytes=16 * 1024 * 1024
+        ),
+    )(own)
+
+
+def scatter_kernel(count, term_ref, sum_ref, xb, ub, db, sb, xs, xr, us, ur, ds, dr):
+    rows, width = sum_ref.shape
+    me, column, line, lines, peer = place(count)
+    step_width = 768 if width % 768 == 0 else 128
+    greet(me, line, lines, peer)
+
+    def across(dest):
+        mine = block_of(term_ref, dest * 2 + 1 - column, rows)
+        return send(mine, xb.at[dest], xs.at[dest], xr.at[dest], peer)
+
+    def upward(dest):
+        return send(sb.at[dest], ub.at[dest], us.at[dest], ur.at[dest], me + 2)
+
+    def downward(dest):
+        return send(sb.at[dest], db.at[dest], ds.at[dest], dr.at[dest], me - 2)
+
+    for away in range(lines - 1, -1, -1):
+
+        @pl.when(line - away >= 0)
+        def _():
+            across(line - away).start()
+
+        if away:
+
+            @pl.when(line + away < lines)
+            def _():
+                across(line + away).start()
+
+    def add(dest, arrived, target, index):
+        first = pl.multiple_of((dest * 2 + column) * rows, rows)
+
+        def some(i, carry):
+            cols = pl.ds(pl.multiple_of(i * step_width, step_width), step_width)
+            total = term_ref[pl.ds(first, rows), cols].astype(jnp.float32)
+            total = total + xb[dest, :, cols].astype(jnp.float32)
+            for ref in arrived:
+                total = total + ref[dest, :, cols].astype(jnp.float32)
+            if index:
+                target[dest, :, cols] = total.astype(target.dtype)
+            else:
+                target[:, cols] = total
+            return carry
+
+        lax.fori_loop(0, width // step_width, some, 0)
+
+    def go_up(dest):
+        @pl.when(dest > line)
+        def _():
+            across(dest).wait_recv()
+
+            @pl.when(line > 0)
+            def _():
+                upward(dest).wait_recv()
+                add(dest, (ub,), sb, True)
+
+            @pl.when(line == 0)
+            def _():
+                add(dest, (), sb, True)
+
+            upward(dest).start()
+
+    def go_down(dest):
+        @pl.when(dest < line)
+        def _():
+            across(dest).wait_recv()
+
+            @pl.when(line < lines - 1)
+            def _():
+                downward(dest).wait_recv()
+                add(dest, (db,), sb, True)
+
+            @pl.when(line == lines - 1)
+            def _():
+                add(dest, (), sb, True)
+
+            downward(dest).start()
+
+    for j in range(lines - 1):
+
+        @pl.when(2 * line < lines)
+        def _():
+            go_up(lines - 1 - j)
+            go_down(j)
+
+        @pl.when(2 * line >= lines)
+        def _():
+            go_down(j)
+            go_up(lines - 1 - j)
+
+    across(line).wait_recv()
+
+    @pl.when(line > 0)
+    def _():
+        upward(line).wait_recv()
+
+    @pl.when(line < lines - 1)
+    def _():
+        downward(line).wait_recv()
+
+    @pl.when((line > 0) & (line < lines - 1))
+    def _():
+        add(line, (ub, db), sum_ref, False)
+
+    @pl.when(line == 0)
+    def _():
+        add(line, (db,), sum_ref, False)
+
+    @pl.when(line == lines - 1)
+    def _():
+        add(line, (ub,), sum_ref, False)
+
+    for dest in range(lines):
+        across(dest).wait_send()
+
+        @pl.when(dest > line)
+        def _():
+            upward(dest).wait_send()
+
+        @pl.when(dest < line)
+        def _():
+            downward(dest).wait_send()
+
+
+def scatter_rows(term):
+    count = lax.axis_size("mp")
+    rows, width = term.shape[0] // count, term.shape[1]
+    if rows % 16 or count % 2 or count < 4:
+        return lax.psum_scatter(term, "mp", scatter_dimension=0, tiled=True)
+    lines = count // 2
+    blocks = pltpu.VMEM((lines, rows, width), jnp.bfloat16)
+    return pl.pallas_call(
+        functools.partial(scatter_kernel, count),
+        out_shape=jax.ShapeDtypeStruct((rows, width), jnp.float32),
+        in_specs=[pl.BlockSpec(memory_space=pltpu.VMEM)],
+        out_specs=pl.BlockSpec(memory_space=pltpu.VMEM),
+        scratch_shapes=[blocks] * 4 + [pltpu.SemaphoreType.DMA((lines,))] * 6,
+        compiler_params=pltpu.CompilerParams(
+            collective_id=1, has_side_effects=True, vmem_limit_bytes=24 * 1024 * 1024
+        ),
+    )(term.astype(jnp.bfloat16))
 
 
 def partner(block, axis, apart):
@@ -111,7 +383,7 @@
     model_count = lax.axis_size("mp")
     model_index = lax.axis_index("mp")
     block_index = lax.axis_index("seq")
-    block_input = lax.all_gather(residual, "mp", axis=0, tiled=True)
+    block_input = gather_rows(residual)
     block_length = block_input.shape[0]
     own_rows = block_length // model_count
     model_width = output_weight.shape[1]
@@ -226,17 +498,12 @@
             picked = lax.dynamic_slice_in_dim(rotated, first_row, row_count, 0)
             return jnp.dot(picked, output_weight, preferred_element_type=jnp.float32)
 
-    attention_rows = lax.psum_scatter(
-        attention_term(jnp.int32(0), lax.axis_size("mp") * own_rows),
-        "mp",
-        scatter_dimension=0,
-        tiled=True,
-    )
+    attention_rows = scatter_rows(attention_term(jnp.int32(0), lax.axis_size("mp") * own_rows))
     first_sum = (residual.astype(jnp.float32) + normalize(attention_rows, attention_gain)).astype(
         jnp.bfloat16
     )
     feed_own = normalize(first_sum, feedforward_gain).astype(jnp.bfloat16)
-    feed_input = lax.all_gather(feed_own, "mp", axis=0, tiled=True)
+    feed_input = gather_rows(feed_own)
     gate_out = jnp.dot(feed_input, gate_weight, preferred_element_type=jnp.float32)
     up_out = jnp.dot(feed_input, up_weight, preferred_element_type=jnp.float32)
     activated = (jax.nn.gelu(gate_out, approximate=True) * up_out).astype(jnp.bfloat16)
@@ -259,12 +526,7 @@
     )
     spread = spread.reshape(block_length, -1)
     picked = spread
-    down_rows = lax.psum_scatter(
-        jnp.dot(picked, down_weight, preferred_element_type=jnp.float32),
-        "mp",
-        scatter_dimension=0,
-        tiled=True,
-    )
+    down_rows = scatter_rows(jnp.dot(picked, down_weight, preferred_element_type=jnp.float32))
     return (first_sum.astype(jnp.float32) + normalize(down_rows, output_gain)).astype(jnp.bfloat16)
 
 

time: 508 us -> 293 us (0.58)
  waiting for transfers between devices: 324 us -> 0.01 us
  Pallas kernels: 0 us -> 139 us
  between operations: 13.5 us -> 0.41 us
  blocking collectives: 79.8 us -> 71.3 us
  other arithmetic: 12.6 us -> 4.38 us
  matrix products: 65.3 us -> 59.5 us
    reduce_scatter x2 -> x0, waiting for transfers between devices: 211 us -> none  [the longest x1 106 us: body(): lax.psum_scatter(attention_term(jnp.int32(0), lax.axis_size('mp') * own_r...]
    pallas_call x0 -> x4, Pallas kernels: none -> 139 us  [the longest x2 70.2 us: scatter_rows(): pl.pallas_call(functools.partial(scatter_kernel, count), out_shape=jax.Sh...]
    all_gather x2 -> x0, waiting for transfers between devices: 112 us -> none  [the longest x1 56.8 us: body(): block_input = lax.all_gather(residual, 'mp', axis=0, tiled=True)]
    all_to_all x1, blocking collectives: 39.8 us -> 33.4 us  [body(): lax.all_to_all(grouped, 'mp', split_axis=0, concat_axis=1, tiled=True)]
    reduce_sum x4, other arithmetic: 6.48 us -> 1.3 us  [normalize(): mean_square = jnp.mean(widened * widened, axis=-1, keepdims=True)]
  transfers between devices with their start and end apart: 6 -> 2, of which waited for: 4 -> 0; matrix products, arithmetic and copies ran while one was open for 1% -> 3% of each run, Pallas kernels for 0% -> 0%
where the time goes in v1:
time: 293 us; the launch traced here: 290 us
  Pallas kernels  139 us (47%)
  blocking collectives  71.3 us (24%)
  matrix products  59.5 us (20%)
  local copies, waits for them, and re-layouts  13.2 us (5%)
  other arithmetic  4.38 us (1%)
    pallas_call x2, Pallas kernels, scatter_rows(): pl.pallas_call(functools.partial(scatter_kernel, count), out_shape=jax.Sh...  70.2 us
    pallas_call x2, Pallas kernels, gather_rows(): pl.pallas_call(functools.partial(gather_kernel, count), out_shape=jax.Sha...  68.5 us
    all_to_all x1, blocking collectives, body(): lax.all_to_all(mixed_rows.astype(jnp.bfloat16), 'mp', split_axis=1, conca...  37.9 us
    all_to_all x1, blocking collectives, body(): lax.all_to_all(grouped, 'mp', split_axis=0, concat_axis=1, tiled=True)  33.4 us
    dot_general x1, matrix products, body(): up_out = jnp.dot(feed_input, up_weight, preferred_element_type=jnp.float32)  15.3 us
    dot_general x1, matrix products, body(): jnp.dot(picked, down_weight, preferred_element_type=jnp.float32)  14.1 us
    dot_general x1, matrix products, body(): jnp.dot(feed_input, gate_weight, preferred_element_type=jnp.float32)  13.5 us
  transfers between devices with their start and end apart: 2, of which 0 were waited for; matrix products, arithmetic and copies ran while one was open for 3% of the time, Pallas kernels for 0%

profile of v1, /device:TPU:0, one launch (start us, length us, event | category | flops | bytes accessed | tf_op | source)
XLA Modules:
  0.0 290.2 jit_solution(15823003321465798378)
XLA Ops:
  0.0 0.8 convert_element_type.91
  0.8 0.5 multiply_cosine_fusion
  1.6 1.0 copy-done.3
  2.5 36.9 %shard_map.136 = bf16[256,5376]{1,0:T(8,128)(2,1)S(1)} custom-call(bf16[32,5376]{1,0:T(8,128)(2,1)S(1)} %copy-done.3), custom_call_target="tpu_custom_call" | custom-call | tf_op jit(solution)/shard_map/pallas_call | solution.py:134
  39.4 0.6 fusion.1
  40.1 1.5 convolution_convert_fusion.4
  41.7 1.3 collective-permute-start.1
  43.0 0.9 convolution_convert_fusion.5
  43.9 1.3 collective-permute-start
  45.3 5.0 %fusion.19 = f32[256,512]{1,0:T(8,128)S(1)} fusion(bf16[5376,512]{1,0:T(8,128)(2,1)} %param.21, bf16[256,5376]{1,0:T(8,128)(2,1)} %copy-done.2, f32[5376]{0:T(1024)S(1)} %copy-done.10, f32[256]{0:T(256)S(1)} %add_rsqrt_fusion), kind=kOutput, calls=%fused_computation.31 | convolution fusion | flops 1415053312 | bytes 8804352 | tf_op jit(solution)/shard_map/dot_general | solution.py:449
  50.3 0.2 copy.62
  50.8 0.2 copy.82
  51.4 0.2 fusion.27
  51.8 2.2 fusion.65
  54.0 2.1 fusion.18
  56.1 4.2 %convolution_convert_fusion.1.term_ref = bf16[256,5376]{1,0:T(8,128)(2,1)S(1)} fusion(bf16[256,512]{0,1:T(8,128)(2,1)S(1)} %bitcast.71, bf16[512,5376]{1,0:T(8,128)(2,1)} %param.24), kind=kOutput, calls=%fused_computation.2 | convolution fusion | flops 1410662400 | bytes 8519680 | tf_op jit(solution)/shard_map/dot_general | solution.py:499
  60.4 37.4 %shard_map.137 = f32[32,5376]{1,0:T(8,128)S(1)} custom-call(bf16[256,5376]{1,0:T(8,128)(2,1)S(1)} %convolution_convert_fusion.1.term_ref), custom_call_target="tpu_custom_call" | custom-call | tf_op jit(solution)/shard_map/pallas_call | solution.py:276
  98.0 0.3 fusion.23
  98.5 31.6 %shard_map.138 = bf16[256,5376]{1,0:T(8,128)(2,1)S(1)} custom-call(bf16[32,5376]{1,0:T(8,128)(2,1)S(1)} %fusion.25.own_ref), custom_call_target="tpu_custom_call" | custom-call | tf_op jit(solution)/shard_map/pallas_call | solution.py:134
  130.2 13.5 %fusion.66 = f32[256,2688]{1,0:T(8,128)S(1)} fusion(bf16[256,5376]{1,0:T(8,128)(2,1)S(1)} %shard_map.138, bf16[5376,2688]{1,0:T(8,128)(2,1)} %param.25), kind=kOutput, calls=%fused_computation.100 | convolution fusion | flops 7398752256 | bytes 34406400 | tf_op jit(solution)/shard_map/dot_general | solution.py:507
  143.7 15.3 %fusion.4 = bf16[256,2688]{1,0:T(8,128)(2,1)} fusion(bf16[256,5376]{1,0:T(8,128)(2,1)S(1)} %shard_map.138, bf16[5376,2688]{1,0:T(8,128)(2,1)} %param.26, f32[256,2688]{1,0:T(8,128)S(1)} %fusion.66), kind=kOutput, calls=%fused_computation.10 | convolution fusion | flops 7405633536 | bytes 35782656 | tf_op jit(solution)/shard_map/dot_general | solution.py:508
  159.0 2.6 copy.69
  161.6 2.2 copy.70
  163.7 33.4 %all_to_all.33 = bf16[256,8,336]{2,1,0:T(8,128)(2,1)S(1)} all-to-all(bf16[256,8,336]{2,1,0:T(8,128)(2,1)S(1)} %copy.70), channel_id=1, replica_groups=mesh['groups'=2,'seq'=2,'mp'=8] {'mp'}, dimensions={0} | all-to-all | bytes 2752512 | tf_op jit(solution)/shard_map/all_to_all | solution.py:518
  197.1 0.6 fusion.15
  197.7 0.9 copy.72
  198.6 37.9 %all_to_all.34 = bf16[32,64,336]{2,0,1:T(8,128)(2,1)S(1)} all-to-all(bf16[32,64,336]{2,0,1:T(8,128)(2,1)S(1)} %copy.72), channel_id=1, replica_groups=mesh['groups'=2,'seq'=2,'mp'=8] {'mp'}, dimensions={1} | all-to-all | bytes 2752512 | tf_op jit(solution)/shard_map/all_to_all | solution.py:524
  236.6 1.7 copy.91
  238.3 3.8 %reshape.195 = bf16[256,2688]{1,0:T(8,128)(2,1)} reshape(bf16[8,32,8,336]{3,2,1,0:T(8,128)(2,1)} %bitcast.68) | data formatting | bytes 2752512 | tf_op jit(solution)/shard_map/reshape | solution.py:527
  242.1 14.1 %convolution_convert_fusion.term_ref = bf16[256,5376]{1,0:T(8,128)(2,1)S(1)} fusion(bf16[256,2688]{1,0:T(8,128)(2,1)} %reshape.195, bf16[2688,5376]{1,0:T(8,128)(2,1)} %param.27), kind=kOutput, calls=%fused_computation.1 | convolution fusion | flops 7400128512 | bytes 33030144 | tf_op jit(solution)/shard_map/dot_general | solution.py:529
  256.3 32.8 %shard_map.139 = f32[32,5376]{1,0:T(8,128)S(1)} custom-call(bf16[256,5376]{1,0:T(8,128)(2,1)S(1)} %convolution_convert_fusion.term_ref), custom_call_target="tpu_custom_call" | custom-call | tf_op jit(solution)/shard_map/pallas_call | solution.py:276
  289.3 0.9 fusion.26
  (45 shorter events, 1.6 us)
Async XLA Ops:
  0.0 40.1 %copy-start = (bf16[5376,256]{1,0:T(8,128)(2,1)S(1)}, bf16[5376,256]{1,0:T(8,128)(2,1)}, u32[]{:S(2)}) copy-start(bf16[5376,256]{1,0:T(8,128)(2,1)} %param.22) | copy-start | bytes 8257540
  1.6 1.0 copy-start.3
  2.5 37.5 %copy-start.10 = (f32[5376]{0:T(1024)S(1)}, f32[5376]{0:T(1024)}, u32[]{:S(2)}) copy-start(f32[5376]{0:T(1024)} %param.17) | copy-start | bytes 64516
  39.4 3.6 %copy-start.2 = (bf16[256,5376]{1,0:T(8,128)(2,1)}, bf16[256,5376]{1,0:T(8,128)(2,1)S(1)}, u32[]{:S(2)}) copy-start(bf16[256,5376]{1,0:T(8,128)(2,1)S(1)} %shard_map.136) | copy-start | bytes 8257540
  40.1 2.9 copy-start.9
  41.7 10.1 %collective-permute-start.1 = (bf16[256,256]{0,1:T(8,128)(2,1)S(1)}, bf16[256,256]{0,1:T(8,128)(2,1)S(1)}, u32[]{:S(2)}, u32[]{:S(2)}) collective-permute-start(bf16[256,256]{0,1:T(8,128)(2,1)S(1)} %bitcast.72), channel_id=1, source_target_pairs={{0,8},{1,9},{2,10},{3,11},{4,12},{5,13},{6,14},{7,15},{16,24},{17,... | collective-permute-start | bytes 393224 | tf_op jit(solution)/shard_map/ppermute | solution.py:305
  43.9 7.7 %collective-permute-start = (bf16[256,256]{1,0:T(8,128)(2,1)S(1)}, bf16[256,256]{1,0:T(8,128)(2,1)S(1)}, u32[]{:S(2)}, u32[]{:S(2)}) collective-permute-start(bf16[256,256]{1,0:T(8,128)(2,1)S(1)} %convolution_convert_fusion.5), channel_id=1, source_target_pairs={{0,8},{1,9},{2,10},{3,11},{4,12},{5,13},{6,14},{7,15},{16,24},{17,... | collective-permute-start | bytes 393224 | tf_op jit(solution)/shard_map/ppermute | solution.py:305
  50.5 0.7 copy-start.8
  60.3 37.7 %copy-start.4 = (bf16[32,5376]{1,0:T(8,128)(2,1)S(1)}, bf16[32,5376]{1,0:T(8,128)(2,1)}, u32[]{:S(2)}) copy-start(bf16[32,5376]{1,0:T(8,128)(2,1)} %own_ref.1) | copy-start | bytes 1032196
  60.3 37.7 %copy-start.6 = (f32[5376]{0:T(1024)S(1)}, f32[5376]{0:T(1024)}, u32[]{:S(2)}) copy-start(f32[5376]{0:T(1024)} %param.18) | copy-start | bytes 64516
  60.3 38.0 %copy-start.5 = (f32[5376]{0:T(1024)S(1)}, f32[5376]{0:T(1024)}, u32[]{:S(2)}) copy-start(f32[5376]{0:T(1024)} %param.19) | copy-start | bytes 64516
  242.1 48.0 %copy-start.1 = (bf16[5376,256]{1,0:T(8,128)(2,1)S(1)}, bf16[5376,256]{1,0:T(8,128)(2,1)}, u32[]{:S(2)}) copy-start(bf16[5376,256]{1,0:T(8,128)(2,1)} %param.22) | copy-start | bytes 8257540
  256.3 33.0 %copy-start.7 = (f32[5376]{0:T(1024)S(1)}, f32[5376]{0:T(1024)}, u32[]{:S(2)}) copy-start(f32[5376]{0:T(1024)} %param.20) | copy-start | bytes 64516

commit v2 on v1

--- a/solution.py
+++ b/solution.py
@@ -283,6 +283,75 @@
             collective_id=1, has_side_effects=True, vmem_limit_bytes=24 * 1024 * 1024
         ),
     )(term.astype(jnp.bfloat16))
+
+
+def hidden_kernel(count, tiles, feed_ref, gate_ref, up_ref, out_ref, act, got, ss, rs):
+    rows = feed_ref.shape[0] // count
+    width = gate_ref.shape[1]
+    tile = pl.program_id(0)
+    me = lax.axis_index("mp")
+
+    @pl.when(tile == 0)
+    def _():
+        barrier = pltpu.get_barrier_semaphore()
+        for k in range(1, count):
+            other = lax.rem(me + k, count)
+            pl.semaphore_signal(barrier, inc=1, device_id={"mp": other}, device_id_type=MESH)
+        pl.semaphore_wait(barrier, count - 1)
+
+    feed = feed_ref[...]
+    gate_out = jnp.dot(feed, gate_ref[...], preferred_element_type=jnp.float32)
+    up_out = jnp.dot(feed, up_ref[...], preferred_element_type=jnp.float32)
+    act[tile] = (jax.nn.gelu(gate_out, approximate=True) * up_out).astype(jnp.bfloat16)
+
+    def to(k, t):
+        other = lax.rem(me + k, count)
+        source = act.at[t, pl.ds(pl.multiple_of(other * rows, rows), rows), :]
+        target = got.at[t, pl.ds(pl.multiple_of(me * rows, rows), rows), :]
+        return send(source, target, ss.at[k, t], rs.at[k, t], other)
+
+    for k in range(1, count):
+        to(k, tile).start()
+    own = pl.ds(pl.multiple_of(me * rows, rows), rows)
+    got[tile, own, :] = act[tile, own, :]
+
+    @pl.when(tile == tiles - 1)
+    def _():
+        for t in range(tiles):
+            for k in range(1, count):
+                to(k, t).wait_recv()
+            out_ref[:, t * width : (t + 1) * width] = got[t]
+        for t in range(tiles):
+            for k in range(1, count):
+                to(k, t).wait_send()
+
+
+def hidden_rows(feed, gate_weight, up_weight):
+    count = lax.axis_size("mp")
+    length, depth = feed.shape
+    hidden = gate_weight.shape[1]
+    rows, tile = length // count, 384
+    tiles = hidden // tile
+    weights = pl.BlockSpec((depth, tile), lambda t: (0, t))
+    return pl.pallas_call(
+        functools.partial(hidden_kernel, count, tiles),
+        grid=(tiles,),
+        out_shape=jax.ShapeDtypeStruct((length, hidden), jnp.bfloat16),
+        in_specs=[pl.BlockSpec((length, depth), lambda t: (0, 0)), weights, weights],
+        out_specs=pl.BlockSpec((length, hidden), lambda t: (0, 0)),
+        scratch_shapes=[
+            pltpu.VMEM((tiles, length, tile), jnp.bfloat16),
+            pltpu.VMEM((tiles, length, tile), jnp.bfloat16),
+            pltpu.SemaphoreType.DMA((count, tiles)),
+            pltpu.SemaphoreType.DMA((count, tiles)),
+        ],
+        compiler_params=pltpu.CompilerParams(
+            collective_id=2,
+            has_side_effects=True,
+            dimension_semantics=("arbitrary",),
+            vmem_limit_bytes=48 * 1024 * 1024,
+        ),
+    )(feed, gate_weight, up_weight)
 
 
 def partner(block, axis, apart):
@@ -504,18 +573,24 @@
     )
     feed_own = normalize(first_sum, feedforward_gain).astype(jnp.bfloat16)
     feed_input = gather_rows(feed_own)
-    gate_out = jnp.dot(feed_input, gate_weight, preferred_element_type=jnp.float32)
-    up_out = jnp.dot(feed_input, up_weight, preferred_element_type=jnp.float32)
-    activated = (jax.nn.gelu(gate_out, approximate=True) * up_out).astype(jnp.bfloat16)
     local_count = WAL // model_count
     block_width = FF // WAL
-    grouped = activated.reshape(block_length, local_count, block_width)
+    if own_rows % 16 == 0 and gate_weight.shape[1] % 384 == 0:
+        gathered = hidden_rows(feed_input, gate_weight, up_weight)
+        gathered = gathered.reshape(model_count, own_rows, local_count, block_width)
+        exchanged = gathered.transpose(1, 0, 2, 3).reshape(own_rows, WAL, block_width)
+    else:
+        gate_out = jnp.dot(feed_input, gate_weight, preferred_element_type=jnp.float32)
+        up_out = jnp.dot(feed_input, up_weight, preferred_element_type=jnp.float32)
+        activated = (jax.nn.gelu(gate_out, approximate=True) * up_out).astype(jnp.bfloat16)
+        grouped = activated.reshape(block_length, local_count, block_width)
+        exchanged = lax.all_to_all(grouped, "mp", split_axis=0, concat_axis=1, tiled=True)
     walsh_scale = float(WAL) ** (-0.5)
     full_table = walsh_table(WAL).astype(jnp.bfloat16)
     mixed_rows = (
         jnp.einsum(
             "rab,ac->rcb",
-            lax.all_to_all(grouped, "mp", split_axis=0, concat_axis=1, tiled=True),
+            exchanged,
             full_table,
             preferred_element_type=jnp.float32,
         )

time: 293 us -> 264 us (0.901)
  Pallas kernels: 139 us -> 175 us
  blocking collectives: 71.3 us -> 39.4 us
  matrix products: 59.5 us -> 30.8 us
  local copies, waits for them, and re-layouts: 13.2 us -> 10.2 us
    pallas_call x0 -> x1, Pallas kernels: none -> 36.8 us  [hidden_rows(): pl.pallas_call(functools.partial(hidden_kernel, count, tiles), grid=(tile...]
    all_to_all x1 -> x0, blocking collectives: 33.4 us -> none  [body(): lax.all_to_all(grouped, 'mp', split_axis=0, concat_axis=1, tiled=True)]
    dot_general x3 -> x1, matrix products: 29.4 us -> 0.58 us  [body(): jnp.einsum('rab,ac->rcb', exchanged, full_table, preferred_element_type=j...]
where the time goes in v2:
time: 264 us; the launch traced here: 263 us
  Pallas kernels  175 us (66%)
  blocking collectives  39.4 us (15%)
  matrix products  30.8 us (12%)
  local copies, waits for them, and re-layouts  10.2 us (4%)
  other arithmetic  4.38 us (2%)
    pallas_call x2, Pallas kernels, scatter_rows(): pl.pallas_call(functools.partial(scatter_kernel, count), out_shape=jax.Sh...  69.7 us
    pallas_call x2, Pallas kernels, gather_rows(): pl.pallas_call(functools.partial(gather_kernel, count), out_shape=jax.Sha...  68.5 us
    all_to_all x1, blocking collectives, body(): lax.all_to_all(mixed_rows.astype(jnp.bfloat16), 'mp', split_axis=1, conca...  39.4 us
    pallas_call x1, Pallas kernels, hidden_rows(): pl.pallas_call(functools.partial(hidden_kernel, count, tiles), grid=(tile...  36.8 us
    dot_general x1, matrix products, body(): jnp.dot(picked, down_weight, preferred_element_type=jnp.float32)  14.3 us
  transfers between devices with their start and end apart: 2, of which 0 were waited for; matrix products, arithmetic and copies ran while one was open for 3% of the time, Pallas kernels for 0%

profile of v2, /device:TPU:0, one launch (start us, length us, event | category | flops | bytes accessed | tf_op | source)
XLA Modules:
  0.0 262.7 jit_solution(4424320702017773064)
XLA Ops:
  0.0 0.8 convert_element_type.88
  0.8 0.5 multiply_cosine_fusion
  1.6 1.0 copy-done.4
  2.5 36.9 %shard_map.136 = bf16[256,5376]{1,0:T(8,128)(2,1)S(1)} custom-call(bf16[32,5376]{1,0:T(8,128)(2,1)S(1)} %copy-done.4), custom_call_target="tpu_custom_call" | custom-call | tf_op jit(solution)/shard_map/pallas_call | solution.py:134
  39.4 0.6 fusion.1
  40.1 1.5 convolution_convert_fusion.4
  41.7 1.3 collective-permute-start.1
  43.0 0.9 convolution_convert_fusion.5
  43.9 1.3 collective-permute-start
  45.3 5.0 %fusion.11 = f32[256,512]{1,0:T(8,128)S(1)} fusion(bf16[5376,512]{1,0:T(8,128)(2,1)} %param.21, bf16[256,5376]{1,0:T(8,128)(2,1)} %copy-done.2, f32[5376]{0:T(1024)S(1)} %copy-done.11, f32[256]{0:T(256)S(1)} %add_rsqrt_fusion), kind=kOutput, calls=%fused_computation.21 | convolution fusion | flops 1415053312 | bytes 8804352 | tf_op jit(solution)/shard_map/dot_general | solution.py:518
  50.3 0.2 copy.46
  50.6 0.2 copy.65
  50.8 0.2 copy.64
  51.4 0.2 fusion.19
  51.8 2.2 fusion.57
  54.0 2.1 fusion.10
  56.1 4.2 %convolution_convert_fusion.1.term_ref = bf16[256,5376]{1,0:T(8,128)(2,1)S(1)} fusion(bf16[256,512]{0,1:T(8,128)(2,1)S(1)} %bitcast.65, bf16[512,5376]{1,0:T(8,128)(2,1)} %param.24), kind=kOutput, calls=%fused_computation.2 | convolution fusion | flops 1410662400 | bytes 8519680 | tf_op jit(solution)/shard_map/dot_general | solution.py:568
  60.3 37.4 %shard_map.137 = f32[32,5376]{1,0:T(8,128)S(1)} custom-call(bf16[256,5376]{1,0:T(8,128)(2,1)S(1)} %convolution_convert_fusion.1.term_ref), custom_call_target="tpu_custom_call" | custom-call | tf_op jit(solution)/shard_map/pallas_call | solution.py:276
  97.8 0.2 multiply_reduce_fusion.1
  98.0 0.3 fusion.15
  98.5 31.6 %shard_map.138.feed_ref = bf16[256,5376]{1,0:T(8,128)(2,1)S(1)} custom-call(bf16[32,5376]{1,0:T(8,128)(2,1)S(1)} %fusion.17.own_ref), custom_call_target="tpu_custom_call" | custom-call | tf_op jit(solution)/shard_map/pallas_call | solution.py:134
  130.1 36.8 %shard_map.139 = bf16[256,2688]{1,0:T(8,128)(2,1)S(1)} custom-call(bf16[256,5376]{1,0:T(8,128)(2,1)S(1)} %shard_map.138.feed_ref, bf16[5376,2688]{1,0:T(8,128)(2,1)} %gate_ref.1, bf16[5376,2688]{1,0:T(8,128)(2,1)} %up_ref.1), custom_call_target="tpu_custom_call" | custom-call | tf_op jit(solution)/shard_map/pallas_call | solution.py:336
  166.9 1.1 copy-done.3
  168.0 3.4 %reshape.197 = bf16[8,32,8,336]{3,2,1,0:T(8,128)(2,1)S(1)} reshape(bf16[256,2688]{1,0:T(8,128)(2,1)} %copy-done.3) | data formatting | bytes 2752512 | tf_op jit(solution)/shard_map/reshape | solution.py:580
  171.4 0.6 fusion.7
  172.0 0.9 copy.54
  172.9 39.4 %all_to_all.15 = bf16[32,64,336]{2,0,1:T(8,128)(2,1)S(1)} all-to-all(bf16[32,64,336]{2,0,1:T(8,128)(2,1)S(1)} %copy.54), channel_id=1, replica_groups=mesh['groups'=2,'seq'=2,'mp'=8] {'mp'}, dimensions={1} | all-to-all | bytes 2752512 | tf_op jit(solution)/shard_map/all_to_all | solution.py:599
  212.3 0.6 copy.73
  212.9 2.1 reshape.199
  215.0 14.3 %convolution_convert_fusion.term_ref = bf16[256,5376]{1,0:T(8,128)(2,1)S(1)} fusion(bf16[256,2688]{1,0:T(8,128)(2,1)} %reshape.199, bf16[2688,5376]{1,0:T(8,128)(2,1)} %param.27), kind=kOutput, calls=%fused_computation.1 | convolution fusion | flops 7400128512 | bytes 33030144 | tf_op jit(solution)/shard_map/dot_general | solution.py:604
  229.3 32.3 %shard_map.140 = f32[32,5376]{1,0:T(8,128)S(1)} custom-call(bf16[256,5376]{1,0:T(8,128)(2,1)S(1)} %convolution_convert_fusion.term_ref), custom_call_target="tpu_custom_call" | custom-call | tf_op jit(solution)/shard_map/pallas_call | solution.py:276
  261.8 0.9 fusion.18
  (44 shorter events, 1.3 us)
Async XLA Ops:
  0.0 40.1 %copy-start = (bf16[5376,256]{1,0:T(8,128)(2,1)S(1)}, bf16[5376,256]{1,0:T(8,128)(2,1)}, u32[]{:S(2)}) copy-start(bf16[5376,256]{1,0:T(8,128)(2,1)} %param.22) | copy-start | bytes 8257540
  1.6 1.0 copy-start.4
  2.5 37.5 %copy-start.11 = (f32[5376]{0:T(1024)S(1)}, f32[5376]{0:T(1024)}, u32[]{:S(2)}) copy-start(f32[5376]{0:T(1024)} %param.17) | copy-start | bytes 64516
  39.4 3.6 %copy-start.2 = (bf16[256,5376]{1,0:T(8,128)(2,1)}, bf16[256,5376]{1,0:T(8,128)(2,1)S(1)}, u32[]{:S(2)}) copy-start(bf16[256,5376]{1,0:T(8,128)(2,1)S(1)} %shard_map.136) | copy-start | bytes 8257540
  40.1 2.9 %copy-start.10 = (bf16[5376,256]{1,0:T(8,128)(2,1)S(1)}, bf16[5376,256]{1,0:T(8,128)(2,1)}, u32[]{:S(2)}) copy-start(bf16[5376,256]{1,0:T(8,128)(2,1)} %param.23) | copy-start | bytes 8257540
  41.7 10.1 %collective-permute-start.1 = (bf16[256,256]{0,1:T(8,128)(2,1)S(1)}, bf16[256,256]{0,1:T(8,128)(2,1)S(1)}, u32[]{:S(2)}, u32[]{:S(2)}) collective-permute-start(bf16[256,256]{0,1:T(8,128)(2,1)S(1)} %bitcast.66), channel_id=1, source_target_pairs={{0,8},{1,9},{2,10},{3,11},{4,12},{5,13},{6,14},{7,15},{16,24},{17,... | collective-permute-start | bytes 393224 | tf_op jit(solution)/shard_map/ppermute | solution.py:374
  43.9 7.7 %collective-permute-start = (bf16[256,256]{1,0:T(8,128)(2,1)S(1)}, bf16[256,256]{1,0:T(8,128)(2,1)S(1)}, u32[]{:S(2)}, u32[]{:S(2)}) collective-permute-start(bf16[256,256]{1,0:T(8,128)(2,1)S(1)} %convolution_convert_fusion.5), channel_id=1, source_target_pairs={{0,8},{1,9},{2,10},{3,11},{4,12},{5,13},{6,14},{7,15},{16,24},{17,... | collective-permute-start | bytes 393224 | tf_op jit(solution)/shard_map/ppermute | solution.py:374
  50.5 0.7 copy-start.9
  60.3 37.7 %copy-start.5 = (bf16[32,5376]{1,0:T(8,128)(2,1)S(1)}, bf16[32,5376]{1,0:T(8,128)(2,1)}, u32[]{:S(2)}) copy-start(bf16[32,5376]{1,0:T(8,128)(2,1)} %own_ref.1) | copy-start | bytes 1032196
  60.3 37.7 %copy-start.7 = (f32[5376]{0:T(1024)S(1)}, f32[5376]{0:T(1024)}, u32[]{:S(2)}) copy-start(f32[5376]{0:T(1024)} %param.18) | copy-start | bytes 64516
  60.3 38.0 %copy-start.6 = (f32[5376]{0:T(1024)S(1)}, f32[5376]{0:T(1024)}, u32[]{:S(2)}) copy-start(f32[5376]{0:T(1024)} %param.19) | copy-start | bytes 64516
  166.9 1.1 copy-start.3
  215.0 47.7 %copy-start.1 = (bf16[5376,256]{1,0:T(8,128)(2,1)S(1)}, bf16[5376,256]{1,0:T(8,128)(2,1)}, u32[]{:S(2)}) copy-start(bf16[5376,256]{1,0:T(8,128)(2,1)} %param.22) | copy-start | bytes 8257540
  229.3 32.5 %copy-start.8 = (f32[5376]{0:T(1024)S(1)}, f32[5376]{0:T(1024)}, u32[]{:S(2)}) copy-start(f32[5376]{0:T(1024)} %param.20) | copy-start | bytes 64516
